TPU v7x, 256 devices: a whole 4x4x8 slice. The times are simulated.
256 devices in a mesh: shot: 4 (over x_hi, core), space: 64 (over x_lo, y, z).
Axes of the slice: x: 4 (x_hi: 2, x_lo: 2; x = x_hi * 2 + x_lo), y: 4, z: 8, core: 2. Of those that a mesh axis runs over, the one named last changes fastest.
Arguments:
- residual_traces: float32 [4, 12, 16384], P('shot', None, 'space'), may hold values from -6 to 6
- owners: int32 [4, 16384, 1], P('shot', 'space'), may hold values from 0 to 63; in each aligned block of 256 rows (0 to 255, 256 to 511, ..., all dimensions but the last counted through in order) at most 8 rows name the same one
- surface_cells: int32 [4, 16384], P('shot', 'space'), may hold values from 0 to 511
- trace_counts: int32 [4], P('shot'), may hold values from 4096 to 16384, as said below
- start_current: float32 [4, 512, 64, 256], P('shot', 'space'), may hold values from -6 to 6
- start_later: float32 [4, 512, 64, 256], P('shot', 'space'), may hold values from -6 to 6
- forward_accel: bfloat16 [4, 12, 512, 64, 256], P('shot', None, 'space'), may hold values from -6 to 6
- courant_sq: float32 [512, 64, 256], P('space'), may hold values from 0.04 to 0.16
Outputs:
- adjoint_field: float32 [4, 512, 64, 256], P('shot', 'space')
- velocity_grad: float32 [512, 64, 256], P('space', 'shot')
Inputs may be any that keep to these rules, and one draw needn't show every extreme that they name: `owners`: among the receivers of one device, no subdomain is named more than 8 times. `trace_counts`: some shot has all 16384 traces live.
All inputs are finite; a program needn't handle non-finite values.
Results may differ from a plain program's by a relative error of at most 0.0003.
Values sent between devices are 32-bit elements; how exact they have to be, the bound alone decides.
A program may use at most 64 MiB of HBM per device.

v0:
```python
import jax
import jax.numpy as jnp
from jax import lax
from jax.sharding import PartitionSpec as P

STENCIL_WEIGHTS = (-205.0 / 72.0, 8.0 / 5.0, -1.0 / 5.0, 8.0 / 315.0, -1.0 / 560.0)


def extended_2(shard, sides, width):
    for axis, dim in sides:
        size, length = (lax.axis_size(axis), shard.shape[dim])
        up = [(i, (i + 1) % size) for i in range(size - 1)]
        down = [(j, i) for i, j in up]
        last = lax.slice_in_dim(shard, length - width, length, axis=dim)
        leading = lax.slice_in_dim(shard, 0, width, axis=dim)
        before = lax.ppermute(last, axis, up)
        after = lax.ppermute(leading, axis, down)
        shard = jnp.concatenate([before, shard, after], axis=dim)
    return shard


def laplace(padded):
    length = padded.shape[0] - 8
    across = padded.shape[1] - 8
    height = padded.shape[2] - 8

    def window(off_x, off_y, off_z):
        return lax.slice(
            padded,
            (4 + off_x, 4 + off_y, 4 + off_z),
            (4 + off_x + length, 4 + off_y + across, 4 + off_z + height),
        )

    summed = 3.0 * STENCIL_WEIGHTS[0] * window(0, 0, 0)
    for offset in range(1, 5):
        six_taps = window(offset, 0, 0) + window(-offset, 0, 0) + window(0, offset, 0)
        six_taps = six_taps + window(0, -offset, 0) + window(0, 0, offset) + window(0, 0, -offset)
        summed = summed + STENCIL_WEIGHTS[offset] * six_taps
    return summed


def laplace_rim(extended):
    return laplace(jnp.pad(extended, ((0, 0), (4, 4), (4, 4))))


def onehot_cells(targets, plane_cells):
    return (targets[:, None] == jnp.arange(plane_cells, dtype=jnp.int32)[None, :]).astype(
        jnp.float32
    )


def shards(
    residual_traces,
    owners,
    surface_cells,
    trace_counts,
    start_current,
    start_later,
    forward_accel,
    courant_sq,
):
    traces = residual_traces[0]
    owner_row = owners[0, :, 0]
    surface = surface_cells[0]
    live_count = trace_counts[0]
    forward = forward_accel[0]
    first_field = start_current[0]
    prior_field = start_later[0]
    length, across, height = courant_sq.shape
    plane_cells = length * across
    steps_all = traces.shape[0]
    my_index = lax.axis_index("space")
    piece_traces = lax.all_gather(traces, "space", axis=1, tiled=True)
    piece_owner = lax.all_gather(owner_row[None, :], "space", axis=1, tiled=True)
    piece_surface = lax.all_gather(surface[None, :], "space", axis=1, tiled=True)
    number = jnp.arange(piece_traces.shape[1], dtype=jnp.int32)
    keep = (number < live_count) & (piece_owner[0] == my_index)
    targets = jnp.where(keep, piece_surface[0], -1)
    table = onehot_cells(targets, plane_cells)
    planes = jnp.dot(
        piece_traces, table, precision=lax.Precision.HIGHEST, preferred_element_type=jnp.float32
    )
    planes = planes.reshape(steps_all, length, across)
    empty = jnp.zeros((length, across, height), jnp.float32)

    def advance(section, state):
        current, later, gradient = state
        extended = extended_2(current, (("space", 0),), 4)
        fresh = 2.0 * current - later + courant_sq * laplace_rim(extended)
        fresh = fresh.at[:, :, 2].add(lax.dynamic_index_in_dim(planes, section, 0, keepdims=False))
        accel = lax.dynamic_index_in_dim(forward, section, 0, keepdims=False).astype(jnp.float32)
        return (fresh, current, gradient + fresh * accel)

    current, later, gradient = lax.fori_loop(
        0, steps_all, advance, (first_field, prior_field, empty)
    )
    velocity_grad = lax.psum_scatter(gradient, "shot", scatter_dimension=1, tiled=True)
    return (current[None], velocity_grad)


def solution(mesh):
    placed = (
        P("shot", None, "space"),
        P("shot", "space", None),
        P("shot", "space"),
        P("shot"),
        P("shot", "space", None, None),
        P("shot", "space", None, None),
        P("shot", None, "space", None, None),
        P("space", None, None),
    )
    return jax.shard_map(
        shards,
        mesh=mesh,
        in_specs=placed,
        out_specs=(P("shot", "space", None, None), P("space", "shot", None)),
        check_vma=False,
    )
```

profile of v0, /device:TPU:1, one launch (start us, length us, event | category | flops | bytes accessed | tf_op | source)
XLA Modules:
  0.0 969.0 jit_solution(18248099924798978966)
XLA Ops:
  7.9 132.5 %all-gather = s32[1,16384,1]{1,2,0:T(1,128)S(1)} all-gather(s32[1,256,1]{1,2,0:T(1,128)} %param.13), channel_id=2, replica_groups=mesh['shot'=4,'space'=64] {'space'}, dimensions={1}, use_global_device_ids=true | all-gather | bytes 66560 | tf_op jit(solution)/shard_map/all_gather | solution.py:74
  140.4 123.0 %all_gather.10 = s32[1,16384]{1,0:T(1,128)S(1)} all-gather(s32[1,256]{1,0:T(1,128)} %param.14), channel_id=1, replica_groups=mesh['shot'=4,'space'=64] {'space'}, dimensions={1}, use_global_device_ids=true | all-gather | bytes 66560 | tf_op jit(solution)/shard_map/all_gather | solution.py:75
  263.4 127.8 %all-gather.1 = f32[1,12,16384]{2,0,1:T(1,128)S(1)} all-gather(f32[1,12,256]{2,0,1:T(1,128)} %param.12), channel_id=3, replica_groups=mesh['shot'=4,'space'=64] {'space'}, dimensions={2}, use_global_device_ids=true | all-gather | bytes 798720 | tf_op jit(solution)/shard_map/all_gather | solution.py:73
  391.4 10.6 %fusion.36 = f32[12,512]{1,0:T(8,128)S(1)} fusion(s32[16384]{0:T(1024)S(1)} %fusion.40, f32[1,12,16384]{2,0,1:T(1,128)S(1)} %all-gather.1), kind=kOutput, calls=%fused_computation.58 | convolution fusion | flops 1216348160 | bytes 876544 | tf_op jit(solution)/shard_map/dot_general | solution.py:80
  405.3 7.0 copy.36
  412.3 383.4 %while.21 = (s32[]{:T(128)}, f32[8,64,256]{1,0,2:T(8,128)S(1)}, f32[8,64,256]{1,0,2:T(8,128)}, f32[8,64,256]{1,0,2:T(8,128)}, f32[8,64,256]{1,0,2:T(8,128)}, /*i...) while((s32[]{:T(128)}, f32[8,64,256]{1,0,2:T(8,128)S(1)}, ...), condition=%wide.region_1.2_spmd.clone, body=%wide.region_0.1_spmd.clone.sunk | while | flops 9936387 | bytes 35305808 | solution.py:94
  427.4 10.2 %fusion.47 = f32[8,64,256]{1,0,2:T(8,128)} fusion(f32[8,64,256]{1,0,2:T(8,128)} %get-tuple-element.335, f32[8,64,256]{1,0,2:T(8,128)S(1)} %get-tuple-element.323, f32[4,64,256]{1,0,2:T(4,128)} %collective-permute-done, f32[16,72,264]{1,0,2:T(8,128)S(1)} %select_maximum_fusion.3, f32[12,64,256]{1,0,2:T(8,128)} %copy-done, ...), kind=kLoop, calls=%fused_computation.25.clone.1 | loop fusion | flops 4849664 | bytes 12845056 | tf_op jit(solution)/shard_map/while/body/eval_jaxpr/add | solution.py:89
  458.9 10.2 %fusion.47 = f32[8,64,256]{1,0,2:T(8,128)} fusion(f32[8,64,256]{1,0,2:T(8,128)} %get-tuple-element.335, f32[8,64,256]{1,0,2:T(8,128)S(1)} %get-tuple-element.323, f32[4,64,256]{1,0,2:T(4,128)} %collective-permute-done, f32[16,72,264]{1,0,2:T(8,128)S(1)} %select_maximum_fusion.3, f32[12,64,256]{1,0,2:T(8,128)} %copy-done, ...), kind=kLoop, calls=%fused_computation.25.clone.1 | loop fusion | flops 4849664 | bytes 12845056 | tf_op jit(solution)/shard_map/while/body/eval_jaxpr/add | solution.py:89
  490.0 10.2 %fusion.47 = f32[8,64,256]{1,0,2:T(8,128)} fusion(f32[8,64,256]{1,0,2:T(8,128)} %get-tuple-element.335, f32[8,64,256]{1,0,2:T(8,128)S(1)} %get-tuple-element.323, f32[4,64,256]{1,0,2:T(4,128)} %collective-permute-done, f32[16,72,264]{1,0,2:T(8,128)S(1)} %select_maximum_fusion.3, f32[12,64,256]{1,0,2:T(8,128)} %copy-done, ...), kind=kLoop, calls=%fused_computation.25.clone.1 | loop fusion | flops 4849664 | bytes 12845056 | tf_op jit(solution)/shard_map/while/body/eval_jaxpr/add | solution.py:89
  521.0 10.2 %fusion.47 = f32[8,64,256]{1,0,2:T(8,128)} fusion(f32[8,64,256]{1,0,2:T(8,128)} %get-tuple-element.335, f32[8,64,256]{1,0,2:T(8,128)S(1)} %get-tuple-element.323, f32[4,64,256]{1,0,2:T(4,128)} %collective-permute-done, f32[16,72,264]{1,0,2:T(8,128)S(1)} %select_maximum_fusion.3, f32[12,64,256]{1,0,2:T(8,128)} %copy-done, ...), kind=kLoop, calls=%fused_computation.25.clone.1 | loop fusion | flops 4849664 | bytes 12845056 | tf_op jit(solution)/shard_map/while/body/eval_jaxpr/add | solution.py:89
  552.1 10.2 %fusion.47 = f32[8,64,256]{1,0,2:T(8,128)} fusion(f32[8,64,256]{1,0,2:T(8,128)} %get-tuple-element.335, f32[8,64,256]{1,0,2:T(8,128)S(1)} %get-tuple-element.323, f32[4,64,256]{1,0,2:T(4,128)} %collective-permute-done, f32[16,72,264]{1,0,2:T(8,128)S(1)} %select_maximum_fusion.3, f32[12,64,256]{1,0,2:T(8,128)} %copy-done, ...), kind=kLoop, calls=%fused_computation.25.clone.1 | loop fusion | flops 4849664 | bytes 12845056 | tf_op jit(solution)/shard_map/while/body/eval_jaxpr/add | solution.py:89
  583.1 10.2 %fusion.47 = f32[8,64,256]{1,0,2:T(8,128)} fusion(f32[8,64,256]{1,0,2:T(8,128)} %get-tuple-element.335, f32[8,64,256]{1,0,2:T(8,128)S(1)} %get-tuple-element.323, f32[4,64,256]{1,0,2:T(4,128)} %collective-permute-done, f32[16,72,264]{1,0,2:T(8,128)S(1)} %select_maximum_fusion.3, f32[12,64,256]{1,0,2:T(8,128)} %copy-done, ...), kind=kLoop, calls=%fused_computation.25.clone.1 | loop fusion | flops 4849664 | bytes 12845056 | tf_op jit(solution)/shard_map/while/body/eval_jaxpr/add | solution.py:89
  614.6 10.2 %fusion.47 = f32[8,64,256]{1,0,2:T(8,128)} fusion(f32[8,64,256]{1,0,2:T(8,128)} %get-tuple-element.335, f32[8,64,256]{1,0,2:T(8,128)S(1)} %get-tuple-element.323, f32[4,64,256]{1,0,2:T(4,128)} %collective-permute-done, f32[16,72,264]{1,0,2:T(8,128)S(1)} %select_maximum_fusion.3, f32[12,64,256]{1,0,2:T(8,128)} %copy-done, ...), kind=kLoop, calls=%fused_computation.25.clone.1 | loop fusion | flops 4849664 | bytes 12845056 | tf_op jit(solution)/shard_map/while/body/eval_jaxpr/add | solution.py:89
  632.5 6.0 collective-permute-start
  646.9 10.2 %fusion.47 = f32[8,64,256]{1,0,2:T(8,128)} fusion(f32[8,64,256]{1,0,2:T(8,128)} %get-tuple-element.335, f32[8,64,256]{1,0,2:T(8,128)S(1)} %get-tuple-element.323, f32[4,64,256]{1,0,2:T(4,128)} %collective-permute-done, f32[16,72,264]{1,0,2:T(8,128)S(1)} %select_maximum_fusion.3, f32[12,64,256]{1,0,2:T(8,128)} %copy-done, ...), kind=kLoop, calls=%fused_computation.25.clone.1 | loop fusion | flops 4849664 | bytes 12845056 | tf_op jit(solution)/shard_map/while/body/eval_jaxpr/add | solution.py:89
  664.8 6.0 collective-permute-start
  679.1 10.2 %fusion.47 = f32[8,64,256]{1,0,2:T(8,128)} fusion(f32[8,64,256]{1,0,2:T(8,128)} %get-tuple-element.335, f32[8,64,256]{1,0,2:T(8,128)S(1)} %get-tuple-element.323, f32[4,64,256]{1,0,2:T(4,128)} %collective-permute-done, f32[16,72,264]{1,0,2:T(8,128)S(1)} %select_maximum_fusion.3, f32[12,64,256]{1,0,2:T(8,128)} %copy-done, ...), kind=kLoop, calls=%fused_computation.25.clone.1 | loop fusion | flops 4849664 | bytes 12845056 | tf_op jit(solution)/shard_map/while/body/eval_jaxpr/add | solution.py:89
  697.1 6.0 collective-permute-start
  711.4 10.2 %fusion.47 = f32[8,64,256]{1,0,2:T(8,128)} fusion(f32[8,64,256]{1,0,2:T(8,128)} %get-tuple-element.335, f32[8,64,256]{1,0,2:T(8,128)S(1)} %get-tuple-element.323, f32[4,64,256]{1,0,2:T(4,128)} %collective-permute-done, f32[16,72,264]{1,0,2:T(8,128)S(1)} %select_maximum_fusion.3, f32[12,64,256]{1,0,2:T(8,128)} %copy-done, ...), kind=kLoop, calls=%fused_computation.25.clone.1 | loop fusion | flops 4849664 | bytes 12845056 | tf_op jit(solution)/shard_map/while/body/eval_jaxpr/add | solution.py:89
  729.3 6.0 collective-permute-start
  744.6 10.2 %fusion.47 = f32[8,64,256]{1,0,2:T(8,128)} fusion(f32[8,64,256]{1,0,2:T(8,128)} %get-tuple-element.335, f32[8,64,256]{1,0,2:T(8,128)S(1)} %get-tuple-element.323, f32[4,64,256]{1,0,2:T(4,128)} %collective-permute-done, f32[16,72,264]{1,0,2:T(8,128)S(1)} %select_maximum_fusion.3, f32[12,64,256]{1,0,2:T(8,128)} %copy-done, ...), kind=kLoop, calls=%fused_computation.25.clone.1 | loop fusion | flops 4849664 | bytes 12845056 | tf_op jit(solution)/shard_map/while/body/eval_jaxpr/add | solution.py:89
  762.5 6.5 collective-permute-start
  779.2 10.2 %fusion.47 = f32[8,64,256]{1,0,2:T(8,128)} fusion(f32[8,64,256]{1,0,2:T(8,128)} %get-tuple-element.335, f32[8,64,256]{1,0,2:T(8,128)S(1)} %get-tuple-element.323, f32[4,64,256]{1,0,2:T(4,128)} %collective-permute-done, f32[16,72,264]{1,0,2:T(8,128)S(1)} %select_maximum_fusion.3, f32[12,64,256]{1,0,2:T(8,128)} %copy-done, ...), kind=kLoop, calls=%fused_computation.25.clone.1 | loop fusion | flops 4849664 | bytes 12845056 | tf_op jit(solution)/shard_map/while/body/eval_jaxpr/add | solution.py:89
  799.2 162.9 %reduce-scatter.2.cloned.1.call-done = f32[8,16,256]{2,1,0:T(8,128)} async-done(((f32[8,64,256]{2,1,0:T(8,128)}), f32[8,16,256]{2,1,0:T(8,128)}) %reduce-scatter.2.cloned.1.call-update) | async-done | bytes 131088 | tf_op jit(solution)/shard_map/reduce_scatter | solution.py:97
  (276 shorter events, 237.1 us)
Async XLA Ops:
  7.2 955.0 %reduce-scatter.2.cloned.1.call-start = ((), (), s32[]{:S(2)}) async-start(), calls=%async_computation.1 | async-start | bytes 655360 | tf_op jit(solution)/shard_map/reduce_scatter | solution.py:97
  412.5 10.4 %collective-permute-start.1 = (f32[4,64,256]{1,0,2:T(4,128)S(1)}, f32[4,64,256]{1,0,2:T(4,128)S(1)}, u32[]{:S(2)}, u32[]{:S(2)}) collective-permute-start(f32[4,64,256]{1,0,2:T(4,128)S(1)} %get-tuple-element.312), channel_id=1, source_target_pairs={{1,0},{2,1},{3,2},{4,3},{5,4},{6,5},{7,6},{8,7},{9,8},{10,9},{11,1... | collective-permute-start | bytes 786440 | tf_op jit(solution)/shard_map/while/body/eval_jaxpr/ppermute | solution.py:17
  413.8 11.3 %collective-permute-start = (f32[4,64,256]{1,0,2:T(4,128)S(1)}, f32[4,64,256]{1,0,2:T(4,128)}, u32[]{:S(2)}, u32[]{:S(2)}) collective-permute-start(f32[4,64,256]{1,0,2:T(4,128)S(1)} %get-tuple-element.311), channel_id=1, source_target_pairs={{0,1},{1,2},{2,3},{3,4},{4,5},{5,6},{6,7},{7,8},{8,9},{9,10},{10,1... | collective-permute-start | bytes 786440 | tf_op jit(solution)/shard_map/while/body/eval_jaxpr/ppermute | solution.py:16
  444.1 10.4 %collective-permute-start.1 = (f32[4,64,256]{1,0,2:T(4,128)S(1)}, f32[4,64,256]{1,0,2:T(4,128)S(1)}, u32[]{:S(2)}, u32[]{:S(2)}) collective-permute-start(f32[4,64,256]{1,0,2:T(4,128)S(1)} %get-tuple-element.312), channel_id=1, source_target_pairs={{1,0},{2,1},{3,2},{4,3},{5,4},{6,5},{7,6},{8,7},{9,8},{10,9},{11,1... | collective-permute-start | bytes 786440 | tf_op jit(solution)/shard_map/while/body/eval_jaxpr/ppermute | solution.py:17
  445.4 11.2 %collective-permute-start = (f32[4,64,256]{1,0,2:T(4,128)S(1)}, f32[4,64,256]{1,0,2:T(4,128)}, u32[]{:S(2)}, u32[]{:S(2)}) collective-permute-start(f32[4,64,256]{1,0,2:T(4,128)S(1)} %get-tuple-element.311), channel_id=1, source_target_pairs={{0,1},{1,2},{2,3},{3,4},{4,5},{5,6},{6,7},{7,8},{8,9},{9,10},{10,1... | collective-permute-start | bytes 786440 | tf_op jit(solution)/shard_map/while/body/eval_jaxpr/ppermute | solution.py:16
  475.5 9.9 %collective-permute-start.1 = (f32[4,64,256]{1,0,2:T(4,128)S(1)}, f32[4,64,256]{1,0,2:T(4,128)S(1)}, u32[]{:S(2)}, u32[]{:S(2)}) collective-permute-start(f32[4,64,256]{1,0,2:T(4,128)S(1)} %get-tuple-element.312), channel_id=1, source_target_pairs={{1,0},{2,1},{3,2},{4,3},{5,4},{6,5},{7,6},{8,7},{9,8},{10,9},{11,1... | collective-permute-start | bytes 786440 | tf_op jit(solution)/shard_map/while/body/eval_jaxpr/ppermute | solution.py:17
  476.8 10.8 %collective-permute-start = (f32[4,64,256]{1,0,2:T(4,128)S(1)}, f32[4,64,256]{1,0,2:T(4,128)}, u32[]{:S(2)}, u32[]{:S(2)}) collective-permute-start(f32[4,64,256]{1,0,2:T(4,128)S(1)} %get-tuple-element.311), channel_id=1, source_target_pairs={{0,1},{1,2},{2,3},{3,4},{4,5},{5,6},{6,7},{7,8},{8,9},{9,10},{10,1... | collective-permute-start | bytes 786440 | tf_op jit(solution)/shard_map/while/body/eval_jaxpr/ppermute | solution.py:16
  506.6 9.9 %collective-permute-start.1 = (f32[4,64,256]{1,0,2:T(4,128)S(1)}, f32[4,64,256]{1,0,2:T(4,128)S(1)}, u32[]{:S(2)}, u32[]{:S(2)}) collective-permute-start(f32[4,64,256]{1,0,2:T(4,128)S(1)} %get-tuple-element.312), channel_id=1, source_target_pairs={{1,0},{2,1},{3,2},{4,3},{5,4},{6,5},{7,6},{8,7},{9,8},{10,9},{11,1... | collective-permute-start | bytes 786440 | tf_op jit(solution)/shard_map/while/body/eval_jaxpr/ppermute | solution.py:17
  507.9 10.8 %collective-permute-start = (f32[4,64,256]{1,0,2:T(4,128)S(1)}, f32[4,64,256]{1,0,2:T(4,128)}, u32[]{:S(2)}, u32[]{:S(2)}) collective-permute-start(f32[4,64,256]{1,0,2:T(4,128)S(1)} %get-tuple-element.311), channel_id=1, source_target_pairs={{0,1},{1,2},{2,3},{3,4},{4,5},{5,6},{6,7},{7,8},{8,9},{9,10},{10,1... | collective-permute-start | bytes 786440 | tf_op jit(solution)/shard_map/while/body/eval_jaxpr/ppermute | solution.py:16
  537.7 9.9 %collective-permute-start.1 = (f32[4,64,256]{1,0,2:T(4,128)S(1)}, f32[4,64,256]{1,0,2:T(4,128)S(1)}, u32[]{:S(2)}, u32[]{:S(2)}) collective-permute-start(f32[4,64,256]{1,0,2:T(4,128)S(1)} %get-tuple-element.312), channel_id=1, source_target_pairs={{1,0},{2,1},{3,2},{4,3},{5,4},{6,5},{7,6},{8,7},{9,8},{10,9},{11,1... | collective-permute-start | bytes 786440 | tf_op jit(solution)/shard_map/while/body/eval_jaxpr/ppermute | solution.py:17
  539.0 10.8 %collective-permute-start = (f32[4,64,256]{1,0,2:T(4,128)S(1)}, f32[4,64,256]{1,0,2:T(4,128)}, u32[]{:S(2)}, u32[]{:S(2)}) collective-permute-start(f32[4,64,256]{1,0,2:T(4,128)S(1)} %get-tuple-element.311), channel_id=1, source_target_pairs={{0,1},{1,2},{2,3},{3,4},{4,5},{5,6},{6,7},{7,8},{8,9},{9,10},{10,1... | collective-permute-start | bytes 786440 | tf_op jit(solution)/shard_map/while/body/eval_jaxpr/ppermute | solution.py:16
  570.0 10.8 %collective-permute-start = (f32[4,64,256]{1,0,2:T(4,128)S(1)}, f32[4,64,256]{1,0,2:T(4,128)}, u32[]{:S(2)}, u32[]{:S(2)}) collective-permute-start(f32[4,64,256]{1,0,2:T(4,128)S(1)} %get-tuple-element.311), channel_id=1, source_target_pairs={{0,1},{1,2},{2,3},{3,4},{4,5},{5,6},{6,7},{7,8},{8,9},{9,10},{10,1... | collective-permute-start | bytes 786440 | tf_op jit(solution)/shard_map/while/body/eval_jaxpr/ppermute | solution.py:16
  599.8 10.3 %collective-permute-start.1 = (f32[4,64,256]{1,0,2:T(4,128)S(1)}, f32[4,64,256]{1,0,2:T(4,128)S(1)}, u32[]{:S(2)}, u32[]{:S(2)}) collective-permute-start(f32[4,64,256]{1,0,2:T(4,128)S(1)} %get-tuple-element.312), channel_id=1, source_target_pairs={{1,0},{2,1},{3,2},{4,3},{5,4},{6,5},{7,6},{8,7},{9,8},{10,9},{11,1... | collective-permute-start | bytes 786440 | tf_op jit(solution)/shard_map/while/body/eval_jaxpr/ppermute | solution.py:17
  601.1 11.2 %collective-permute-start = (f32[4,64,256]{1,0,2:T(4,128)S(1)}, f32[4,64,256]{1,0,2:T(4,128)}, u32[]{:S(2)}, u32[]{:S(2)}) collective-permute-start(f32[4,64,256]{1,0,2:T(4,128)S(1)} %get-tuple-element.311), channel_id=1, source_target_pairs={{0,1},{1,2},{2,3},{3,4},{4,5},{5,6},{6,7},{7,8},{8,9},{9,10},{10,1... | collective-permute-start | bytes 786440 | tf_op jit(solution)/shard_map/while/body/eval_jaxpr/ppermute | solution.py:16
  631.2 11.1 %collective-permute-start.1 = (f32[4,64,256]{1,0,2:T(4,128)S(1)}, f32[4,64,256]{1,0,2:T(4,128)S(1)}, u32[]{:S(2)}, u32[]{:S(2)}) collective-permute-start(f32[4,64,256]{1,0,2:T(4,128)S(1)} %get-tuple-element.312), channel_id=1, source_target_pairs={{1,0},{2,1},{3,2},{4,3},{5,4},{6,5},{7,6},{8,7},{9,8},{10,9},{11,1... | collective-permute-start | bytes 786440 | tf_op jit(solution)/shard_map/while/body/eval_jaxpr/ppermute | solution.py:17
  632.5 12.0 %collective-permute-start = (f32[4,64,256]{1,0,2:T(4,128)S(1)}, f32[4,64,256]{1,0,2:T(4,128)}, u32[]{:S(2)}, u32[]{:S(2)}) collective-permute-start(f32[4,64,256]{1,0,2:T(4,128)S(1)} %get-tuple-element.311), channel_id=1, source_target_pairs={{0,1},{1,2},{2,3},{3,4},{4,5},{5,6},{6,7},{7,8},{8,9},{9,10},{10,1... | collective-permute-start | bytes 786440 | tf_op jit(solution)/shard_map/while/body/eval_jaxpr/ppermute | solution.py:16
  663.5 11.1 %collective-permute-start.1 = (f32[4,64,256]{1,0,2:T(4,128)S(1)}, f32[4,64,256]{1,0,2:T(4,128)S(1)}, u32[]{:S(2)}, u32[]{:S(2)}) collective-permute-start(f32[4,64,256]{1,0,2:T(4,128)S(1)} %get-tuple-element.312), channel_id=1, source_target_pairs={{1,0},{2,1},{3,2},{4,3},{5,4},{6,5},{7,6},{8,7},{9,8},{10,9},{11,1... | collective-permute-start | bytes 786440 | tf_op jit(solution)/shard_map/while/body/eval_jaxpr/ppermute | solution.py:17
  664.8 12.0 %collective-permute-start = (f32[4,64,256]{1,0,2:T(4,128)S(1)}, f32[4,64,256]{1,0,2:T(4,128)}, u32[]{:S(2)}, u32[]{:S(2)}) collective-permute-start(f32[4,64,256]{1,0,2:T(4,128)S(1)} %get-tuple-element.311), channel_id=1, source_target_pairs={{0,1},{1,2},{2,3},{3,4},{4,5},{5,6},{6,7},{7,8},{8,9},{9,10},{10,1... | collective-permute-start | bytes 786440 | tf_op jit(solution)/shard_map/while/body/eval_jaxpr/ppermute | solution.py:16
  695.8 11.1 %collective-permute-start.1 = (f32[4,64,256]{1,0,2:T(4,128)S(1)}, f32[4,64,256]{1,0,2:T(4,128)S(1)}, u32[]{:S(2)}, u32[]{:S(2)}) collective-permute-start(f32[4,64,256]{1,0,2:T(4,128)S(1)} %get-tuple-element.312), channel_id=1, source_target_pairs={{1,0},{2,1},{3,2},{4,3},{5,4},{6,5},{7,6},{8,7},{9,8},{10,9},{11,1... | collective-permute-start | bytes 786440 | tf_op jit(solution)/shard_map/while/body/eval_jaxpr/ppermute | solution.py:17
  697.1 12.0 %collective-permute-start = (f32[4,64,256]{1,0,2:T(4,128)S(1)}, f32[4,64,256]{1,0,2:T(4,128)}, u32[]{:S(2)}, u32[]{:S(2)}) collective-permute-start(f32[4,64,256]{1,0,2:T(4,128)S(1)} %get-tuple-element.311), channel_id=1, source_target_pairs={{0,1},{1,2},{2,3},{3,4},{4,5},{5,6},{6,7},{7,8},{8,9},{9,10},{10,1... | collective-permute-start | bytes 786440 | tf_op jit(solution)/shard_map/while/body/eval_jaxpr/ppermute | solution.py:16
  728.0 12.0 %collective-permute-start.1 = (f32[4,64,256]{1,0,2:T(4,128)S(1)}, f32[4,64,256]{1,0,2:T(4,128)S(1)}, u32[]{:S(2)}, u32[]{:S(2)}) collective-permute-start(f32[4,64,256]{1,0,2:T(4,128)S(1)} %get-tuple-element.312), channel_id=1, source_target_pairs={{1,0},{2,1},{3,2},{4,3},{5,4},{6,5},{7,6},{8,7},{9,8},{10,9},{11,1... | collective-permute-start | bytes 786440 | tf_op jit(solution)/shard_map/while/body/eval_jaxpr/ppermute | solution.py:17
  729.3 12.9 %collective-permute-start = (f32[4,64,256]{1,0,2:T(4,128)S(1)}, f32[4,64,256]{1,0,2:T(4,128)}, u32[]{:S(2)}, u32[]{:S(2)}) collective-permute-start(f32[4,64,256]{1,0,2:T(4,128)S(1)} %get-tuple-element.311), channel_id=1, source_target_pairs={{0,1},{1,2},{2,3},{3,4},{4,5},{5,6},{6,7},{7,8},{8,9},{9,10},{10,1... | collective-permute-start | bytes 786440 | tf_op jit(solution)/shard_map/while/body/eval_jaxpr/ppermute | solution.py:16
  761.2 13.5 %collective-permute-start.1 = (f32[4,64,256]{1,0,2:T(4,128)S(1)}, f32[4,64,256]{1,0,2:T(4,128)S(1)}, u32[]{:S(2)}, u32[]{:S(2)}) collective-permute-start(f32[4,64,256]{1,0,2:T(4,128)S(1)} %get-tuple-element.312), channel_id=1, source_target_pairs={{1,0},{2,1},{3,2},{4,3},{5,4},{6,5},{7,6},{8,7},{9,8},{10,9},{11,1... | collective-permute-start | bytes 786440 | tf_op jit(solution)/shard_map/while/body/eval_jaxpr/ppermute | solution.py:17
  762.5 14.4 %collective-permute-start = (f32[4,64,256]{1,0,2:T(4,128)S(1)}, f32[4,64,256]{1,0,2:T(4,128)}, u32[]{:S(2)}, u32[]{:S(2)}) collective-permute-start(f32[4,64,256]{1,0,2:T(4,128)S(1)} %get-tuple-element.311), channel_id=1, source_target_pairs={{0,1},{1,2},{2,3},{3,4},{4,5},{5,6},{6,7},{7,8},{8,9},{9,10},{10,1... | collective-permute-start | bytes 786440 | tf_op jit(solution)/shard_map/while/body/eval_jaxpr/ppermute | solution.py:16
  (64 other events, 132.7 us)
Sparse Core Ops, SparseCore 0:
  798.2 163.8 reduce-scatter.1
where the time goes:
time: 971 us; the launch traced here: 969 us
  blocking collectives  383 us (39%)
  waiting for transfers between devices  211 us (22%)
  other arithmetic  184 us (19%)
  local copies, waits for them, and re-layouts  84.5 us (9%)
  starting transfers between devices  80.2 us (8%)
  between operations  14.7 us (2%)
  matrix products  10.6 us (1%)
    reduce_scatter x1, waiting for transfers between devices, shards(): lax.psum_scatter(gradient, 'shot', scatter_dimension=1, tiled=True)  163 us
    all_gather x1, blocking collectives, shards(): lax.all_gather(owner_row[None, :], 'space', axis=1, tiled=True)  133 us
    all_gather x1, blocking collectives, shards(): piece_traces = lax.all_gather(traces, 'space', axis=1, tiled=True)  128 us
    all_gather x1, blocking collectives, shards(): lax.all_gather(surface[None, :], 'space', axis=1, tiled=True)  123 us
    add x12, other arithmetic, advance(): fresh = 2.0 * current - later + courant_sq * laplace_rim(extended)  122 us
    while x156, local copies, waits for them, and re-layouts  67.3 us
    ppermute x12, starting transfers between devices, extended_2(): before = lax.ppermute(last, axis, up)  64.7 us
    ppermute x12, waiting for transfers between devices, extended_2(): after = lax.ppermute(leading, axis, down)  48.5 us
  transfers between devices with their start and end apart: 25, of which 13 were waited for; matrix products, arithmetic and copies ran while one was open for 0% of the time, Pallas kernels for 0%

commit v1 on v0

--- a/solution.py
+++ b/solution.py
@@ -4,6 +4,14 @@
 from jax.sharding import PartitionSpec as P
 
 STENCIL_WEIGHTS = (-205.0 / 72.0, 8.0 / 5.0, -1.0 / 5.0, 8.0 / 315.0, -1.0 / 560.0)
+
+
+def switch_ladders(mine_x, which_axis, row_dim):
+    block_last = jnp.concatenate(
+        lax.all_to_all(jnp.stack([mine_x] * lax.axis_size(which_axis)), which_axis, 0, 0),
+        axis=row_dim,
+    )
+    return block_last
 
 
 def extended_2(shard, sides, width):
@@ -72,7 +80,7 @@
     my_index = lax.axis_index("space")
     piece_traces = lax.all_gather(traces, "space", axis=1, tiled=True)
     piece_owner = lax.all_gather(owner_row[None, :], "space", axis=1, tiled=True)
-    piece_surface = lax.all_gather(surface[None, :], "space", axis=1, tiled=True)
+    piece_surface = switch_ladders(surface[None, :], "space", 1)
     number = jnp.arange(piece_traces.shape[1], dtype=jnp.int32)
     keep = (number < live_count) & (piece_owner[0] == my_index)
     targets = jnp.where(keep, piece_surface[0], -1)

time: 971 us -> 837 us (0.86)
  blocking collectives: 383 us -> 255 us
  waiting for transfers between devices: 211 us -> 186 us
  starting transfers between devices: 80.2 us -> 95.5 us
    all_gather x1 -> x0, blocking collectives: 123 us -> none  [shards(): lax.all_gather(surface[None, :], 'space', axis=1, tiled=True)]
    reduce_scatter x1, waiting for transfers between devices: 163 us -> 108 us  [shards(): lax.psum_scatter(gradient, 'shot', scatter_dimension=1, tiled=True)]
    ppermute x12, waiting for transfers between devices: 48.5 us -> 77.9 us  [extended_2(): after = lax.ppermute(leading, axis, down)]
    all_to_all x0 -> x1, starting transfers between devices: none -> 13.6 us  [switch_ladders(): lax.all_to_all(jnp.stack([mine_x] * lax.axis_size(which_axis)), which_axi...]
    all_gather x1, blocking collectives: 133 us -> 123 us  [shards(): lax.all_gather(owner_row[None, :], 'space', axis=1, tiled=True)]
  transfers between devices with their start and end apart: 25 -> 26, of which waited for: 13 -> 13; matrix products, arithmetic and copies ran while one was open for 0% -> 2% of each run, Pallas kernels for 0% -> 0%
where the time goes in v1:
time: 837 us; the launch traced here: 834 us
  blocking collectives  255 us (30%)
  waiting for transfers between devices  186 us (22%)
  other arithmetic  185 us (22%)
  starting transfers between devices  95.5 us (11%)
  local copies, waits for them, and re-layouts  86.4 us (10%)
  between operations  14.7 us (2%)
  matrix products  10.6 us (1%)
    all_gather x1, blocking collectives, shards(): piece_traces = lax.all_gather(traces, 'space', axis=1, tiled=True)  133 us
    add x12, other arithmetic, advance(): fresh = 2.0 * current - later + courant_sq * laplace_rim(extended)  123 us
    all_gather x1, blocking collectives, shards(): lax.all_gather(owner_row[None, :], 'space', axis=1, tiled=True)  123 us
    reduce_scatter x1, waiting for transfers between devices, shards(): lax.psum_scatter(gradient, 'shot', scatter_dimension=1, tiled=True)  108 us
    ppermute x12, waiting for transfers between devices, extended_2(): after = lax.ppermute(leading, axis, down)  77.9 us
    while x156, local copies, waits for them, and re-layouts  66.7 us
    ppermute x12, starting transfers between devices, extended_2(): before = lax.ppermute(last, axis, up)  66.3 us
    concatenate x12, other arithmetic, extended_2(): shard = jnp.concatenate([before, shard, after], axis=dim)  28.2 us
  transfers between devices with their start and end apart: 26, of which 13 were waited for; matrix products, arithmetic and copies ran while one was open for 2% of the time, Pallas kernels for 0%

profile of v1, /device:TPU:1, one launch (start us, length us, event | category | flops | bytes accessed | tf_op | source)
XLA Modules:
  0.0 834.2 jit_solution(7289668024525152601)
XLA Ops:
  8.6 13.6 %all-to-all-start = ((s32[64,1,256]{2,1,0:T(1,128)}), s32[64,1,256]{2,1,0:T(1,128)S(1)}, u32[]{:S(2)}, u32[]{:S(2)}) async-start(s32[64,1,256]{2,1,0:T(1,128)} %stack.3), calls=%async_computation | async-start | bytes 131072 | tf_op jit(solution)/shard_map/all_to_all | solution.py:11
  22.3 132.8 %all-gather.1 = f32[1,12,16384]{2,0,1:T(1,128)S(1)} all-gather(f32[1,12,256]{2,0,1:T(1,128)} %param.12), channel_id=3, replica_groups=mesh['shot'=4,'space'=64] {'space'}, dimensions={2}, use_global_device_ids=true | all-gather | bytes 798720 | tf_op jit(solution)/shard_map/all_gather | solution.py:81
  155.0 122.6 %all-gather = s32[1,16384,1]{1,2,0:T(1,128)S(1)} all-gather(s32[1,256,1]{1,2,0:T(1,128)} %param.13), channel_id=2, replica_groups=mesh['shot'=4,'space'=64] {'space'}, dimensions={1}, use_global_device_ids=true | all-gather | bytes 66560 | tf_op jit(solution)/shard_map/all_gather | solution.py:82
  289.8 10.6 %fusion.36 = f32[12,512]{1,0:T(8,128)S(1)} fusion(s32[16384]{0:T(1024)S(1)} %fusion.40, f32[1,12,16384]{2,0,1:T(1,128)S(1)} %all-gather.1), kind=kOutput, calls=%fused_computation.58 | convolution fusion | flops 1216348160 | bytes 876544 | tf_op jit(solution)/shard_map/dot_general | solution.py:88
  300.4 415.0 %while.21 = (s32[]{:T(128)}, f32[8,64,256]{1,0,2:T(8,128)S(1)}, f32[8,64,256]{1,0,2:T(8,128)}, f32[8,64,256]{1,0,2:T(8,128)}, f32[8,64,256]{1,0,2:T(8,128)}, /*i...) while((s32[]{:T(128)}, f32[8,64,256]{1,0,2:T(8,128)S(1)}, ...), condition=%wide.region_1.2_spmd.clone, body=%wide.region_0.1_spmd.clone.sunk | while | flops 9936387 | bytes 35305808 | solution.py:102
  315.4 10.2 %fusion.47 = f32[8,64,256]{1,0,2:T(8,128)} fusion(f32[8,64,256]{1,0,2:T(8,128)} %get-tuple-element.335, f32[8,64,256]{1,0,2:T(8,128)S(1)} %get-tuple-element.323, f32[4,64,256]{1,0,2:T(4,128)} %collective-permute-done, f32[16,72,264]{1,0,2:T(8,128)S(1)} %select_maximum_fusion.3, f32[12,64,256]{1,0,2:T(8,128)} %copy-done, ...), kind=kLoop, calls=%fused_computation.25.clone.1 | loop fusion | flops 4849664 | bytes 12845056 | tf_op jit(solution)/shard_map/while/body/eval_jaxpr/add | solution.py:97
  346.6 10.2 %fusion.47 = f32[8,64,256]{1,0,2:T(8,128)} fusion(f32[8,64,256]{1,0,2:T(8,128)} %get-tuple-element.335, f32[8,64,256]{1,0,2:T(8,128)S(1)} %get-tuple-element.323, f32[4,64,256]{1,0,2:T(4,128)} %collective-permute-done, f32[16,72,264]{1,0,2:T(8,128)S(1)} %select_maximum_fusion.3, f32[12,64,256]{1,0,2:T(8,128)} %copy-done, ...), kind=kLoop, calls=%fused_computation.25.clone.1 | loop fusion | flops 4849664 | bytes 12845056 | tf_op jit(solution)/shard_map/while/body/eval_jaxpr/add | solution.py:97
  377.7 10.2 %fusion.47 = f32[8,64,256]{1,0,2:T(8,128)} fusion(f32[8,64,256]{1,0,2:T(8,128)} %get-tuple-element.335, f32[8,64,256]{1,0,2:T(8,128)S(1)} %get-tuple-element.323, f32[4,64,256]{1,0,2:T(4,128)} %collective-permute-done, f32[16,72,264]{1,0,2:T(8,128)S(1)} %select_maximum_fusion.3, f32[12,64,256]{1,0,2:T(8,128)} %copy-done, ...), kind=kLoop, calls=%fused_computation.25.clone.1 | loop fusion | flops 4849664 | bytes 12845056 | tf_op jit(solution)/shard_map/while/body/eval_jaxpr/add | solution.py:97
  410.0 10.2 %fusion.47 = f32[8,64,256]{1,0,2:T(8,128)} fusion(f32[8,64,256]{1,0,2:T(8,128)} %get-tuple-element.335, f32[8,64,256]{1,0,2:T(8,128)S(1)} %get-tuple-element.323, f32[4,64,256]{1,0,2:T(4,128)} %collective-permute-done, f32[16,72,264]{1,0,2:T(8,128)S(1)} %select_maximum_fusion.3, f32[12,64,256]{1,0,2:T(8,128)} %copy-done, ...), kind=kLoop, calls=%fused_computation.25.clone.1 | loop fusion | flops 4849664 | bytes 12845056 | tf_op jit(solution)/shard_map/while/body/eval_jaxpr/add | solution.py:97
  443.4 10.2 %fusion.47 = f32[8,64,256]{1,0,2:T(8,128)} fusion(f32[8,64,256]{1,0,2:T(8,128)} %get-tuple-element.335, f32[8,64,256]{1,0,2:T(8,128)S(1)} %get-tuple-element.323, f32[4,64,256]{1,0,2:T(4,128)} %collective-permute-done, f32[16,72,264]{1,0,2:T(8,128)S(1)} %select_maximum_fusion.3, f32[12,64,256]{1,0,2:T(8,128)} %copy-done, ...), kind=kLoop, calls=%fused_computation.25.clone.1 | loop fusion | flops 4849664 | bytes 12845056 | tf_op jit(solution)/shard_map/while/body/eval_jaxpr/add | solution.py:97
  478.0 10.2 %fusion.47 = f32[8,64,256]{1,0,2:T(8,128)} fusion(f32[8,64,256]{1,0,2:T(8,128)} %get-tuple-element.335, f32[8,64,256]{1,0,2:T(8,128)S(1)} %get-tuple-element.323, f32[4,64,256]{1,0,2:T(4,128)} %collective-permute-done, f32[16,72,264]{1,0,2:T(8,128)S(1)} %select_maximum_fusion.3, f32[12,64,256]{1,0,2:T(8,128)} %copy-done, ...), kind=kLoop, calls=%fused_computation.25.clone.1 | loop fusion | flops 4849664 | bytes 12845056 | tf_op jit(solution)/shard_map/while/body/eval_jaxpr/add | solution.py:97
  501.3 7.7 collective-permute-done.1
  513.5 10.2 %fusion.47 = f32[8,64,256]{1,0,2:T(8,128)} fusion(f32[8,64,256]{1,0,2:T(8,128)} %get-tuple-element.335, f32[8,64,256]{1,0,2:T(8,128)S(1)} %get-tuple-element.323, f32[4,64,256]{1,0,2:T(4,128)} %collective-permute-done, f32[16,72,264]{1,0,2:T(8,128)S(1)} %select_maximum_fusion.3, f32[12,64,256]{1,0,2:T(8,128)} %copy-done, ...), kind=kLoop, calls=%fused_computation.25.clone.1 | loop fusion | flops 4849664 | bytes 12845056 | tf_op jit(solution)/shard_map/while/body/eval_jaxpr/add | solution.py:97
  537.6 8.0 collective-permute-done.1
  550.1 10.2 %fusion.47 = f32[8,64,256]{1,0,2:T(8,128)} fusion(f32[8,64,256]{1,0,2:T(8,128)} %get-tuple-element.335, f32[8,64,256]{1,0,2:T(8,128)S(1)} %get-tuple-element.323, f32[4,64,256]{1,0,2:T(4,128)} %collective-permute-done, f32[16,72,264]{1,0,2:T(8,128)S(1)} %select_maximum_fusion.3, f32[12,64,256]{1,0,2:T(8,128)} %copy-done, ...), kind=kLoop, calls=%fused_computation.25.clone.1 | loop fusion | flops 4849664 | bytes 12845056 | tf_op jit(solution)/shard_map/while/body/eval_jaxpr/add | solution.py:97
  575.2 9.5 %collective-permute-done.1 = f32[4,64,256]{1,0,2:T(4,128)S(1)} collective-permute-done((f32[4,64,256]{1,0,2:T(4,128)S(1)}, f32[4,64,256]{1,0,2:T(4,128)S(1)}, u32[]{:S(2)}, u32[]{:S(2)}) %collective-permute-start.1) | collective-permute-done | bytes 262176 | tf_op jit(solution)/shard_map/while/body/eval_jaxpr/ppermute | solution.py:25
  589.1 10.2 %fusion.47 = f32[8,64,256]{1,0,2:T(8,128)} fusion(f32[8,64,256]{1,0,2:T(8,128)} %get-tuple-element.335, f32[8,64,256]{1,0,2:T(8,128)S(1)} %get-tuple-element.323, f32[4,64,256]{1,0,2:T(4,128)} %collective-permute-done, f32[16,72,264]{1,0,2:T(8,128)S(1)} %select_maximum_fusion.3, f32[12,64,256]{1,0,2:T(8,128)} %copy-done, ...), kind=kLoop, calls=%fused_computation.25.clone.1 | loop fusion | flops 4849664 | bytes 12845056 | tf_op jit(solution)/shard_map/while/body/eval_jaxpr/add | solution.py:97
  614.2 8.9 %collective-permute-done.1 = f32[4,64,256]{1,0,2:T(4,128)S(1)} collective-permute-done((f32[4,64,256]{1,0,2:T(4,128)S(1)}, f32[4,64,256]{1,0,2:T(4,128)S(1)}, u32[]{:S(2)}, u32[]{:S(2)}) %collective-permute-start.1) | collective-permute-done | bytes 262176 | tf_op jit(solution)/shard_map/while/body/eval_jaxpr/ppermute | solution.py:25
  627.6 10.2 %fusion.47 = f32[8,64,256]{1,0,2:T(8,128)} fusion(f32[8,64,256]{1,0,2:T(8,128)} %get-tuple-element.335, f32[8,64,256]{1,0,2:T(8,128)S(1)} %get-tuple-element.323, f32[4,64,256]{1,0,2:T(4,128)} %collective-permute-done, f32[16,72,264]{1,0,2:T(8,128)S(1)} %select_maximum_fusion.3, f32[12,64,256]{1,0,2:T(8,128)} %copy-done, ...), kind=kLoop, calls=%fused_computation.25.clone.1 | loop fusion | flops 4849664 | bytes 12845056 | tf_op jit(solution)/shard_map/while/body/eval_jaxpr/add | solution.py:97
  651.8 8.1 collective-permute-done.1
  664.4 10.2 %fusion.47 = f32[8,64,256]{1,0,2:T(8,128)} fusion(f32[8,64,256]{1,0,2:T(8,128)} %get-tuple-element.335, f32[8,64,256]{1,0,2:T(8,128)S(1)} %get-tuple-element.323, f32[4,64,256]{1,0,2:T(4,128)} %collective-permute-done, f32[16,72,264]{1,0,2:T(8,128)S(1)} %select_maximum_fusion.3, f32[12,64,256]{1,0,2:T(8,128)} %copy-done, ...), kind=kLoop, calls=%fused_computation.25.clone.1 | loop fusion | flops 4849664 | bytes 12845056 | tf_op jit(solution)/shard_map/while/body/eval_jaxpr/add | solution.py:97
  687.3 7.2 collective-permute-done.1
  698.9 10.2 %fusion.47 = f32[8,64,256]{1,0,2:T(8,128)} fusion(f32[8,64,256]{1,0,2:T(8,128)} %get-tuple-element.335, f32[8,64,256]{1,0,2:T(8,128)S(1)} %get-tuple-element.323, f32[4,64,256]{1,0,2:T(4,128)} %collective-permute-done, f32[16,72,264]{1,0,2:T(8,128)S(1)} %select_maximum_fusion.3, f32[12,64,256]{1,0,2:T(8,128)} %copy-done, ...), kind=kLoop, calls=%fused_computation.25.clone.1 | loop fusion | flops 4849664 | bytes 12845056 | tf_op jit(solution)/shard_map/while/body/eval_jaxpr/add | solution.py:97
  719.0 108.4 %reduce-scatter.2.cloned.1.call-done = f32[8,16,256]{2,1,0:T(8,128)} async-done(((f32[8,64,256]{2,1,0:T(8,128)}), f32[8,16,256]{2,1,0:T(8,128)}) %reduce-scatter.2.cloned.1.call-update) | async-done | bytes 131088 | tf_op jit(solution)/shard_map/reduce_scatter | solution.py:105
  (276 shorter events, 258.6 us)
Async XLA Ops:
  8.6 281.1 %all-to-all-start = ((s32[64,1,256]{2,1,0:T(1,128)}), s32[64,1,256]{2,1,0:T(1,128)S(1)}, u32[]{:S(2)}, u32[]{:S(2)}) async-start(s32[64,1,256]{2,1,0:T(1,128)} %stack.3), calls=%async_computation | async-start | bytes 131072 | tf_op jit(solution)/shard_map/all_to_all | solution.py:11
  22.2 805.2 %reduce-scatter.2.cloned.1.call-start = ((), (), s32[]{:S(2)}) async-start(), calls=%async_computation.2 | async-start | bytes 655360 | tf_op jit(solution)/shard_map/reduce_scatter | solution.py:105
  300.8 10.1 %collective-permute-start.1 = (f32[4,64,256]{1,0,2:T(4,128)S(1)}, f32[4,64,256]{1,0,2:T(4,128)S(1)}, u32[]{:S(2)}, u32[]{:S(2)}) collective-permute-start(f32[4,64,256]{1,0,2:T(4,128)S(1)} %get-tuple-element.312), channel_id=1, source_target_pairs={{1,0},{2,1},{3,2},{4,3},{5,4},{6,5},{7,6},{8,7},{9,8},{10,9},{11,1... | collective-permute-start | bytes 786440 | tf_op jit(solution)/shard_map/while/body/eval_jaxpr/ppermute | solution.py:25
  302.1 11.0 %collective-permute-start = (f32[4,64,256]{1,0,2:T(4,128)S(1)}, f32[4,64,256]{1,0,2:T(4,128)}, u32[]{:S(2)}, u32[]{:S(2)}) collective-permute-start(f32[4,64,256]{1,0,2:T(4,128)S(1)} %get-tuple-element.311), channel_id=1, source_target_pairs={{0,1},{1,2},{2,3},{3,4},{4,5},{5,6},{6,7},{7,8},{8,9},{9,10},{10,1... | collective-permute-start | bytes 786440 | tf_op jit(solution)/shard_map/while/body/eval_jaxpr/ppermute | solution.py:24
  333.4 10.9 %collective-permute-start = (f32[4,64,256]{1,0,2:T(4,128)S(1)}, f32[4,64,256]{1,0,2:T(4,128)}, u32[]{:S(2)}, u32[]{:S(2)}) collective-permute-start(f32[4,64,256]{1,0,2:T(4,128)S(1)} %get-tuple-element.311), channel_id=1, source_target_pairs={{0,1},{1,2},{2,3},{3,4},{4,5},{5,6},{6,7},{7,8},{8,9},{9,10},{10,1... | collective-permute-start | bytes 786440 | tf_op jit(solution)/shard_map/while/body/eval_jaxpr/ppermute | solution.py:24
  364.6 10.8 %collective-permute-start = (f32[4,64,256]{1,0,2:T(4,128)S(1)}, f32[4,64,256]{1,0,2:T(4,128)}, u32[]{:S(2)}, u32[]{:S(2)}) collective-permute-start(f32[4,64,256]{1,0,2:T(4,128)S(1)} %get-tuple-element.311), channel_id=1, source_target_pairs={{0,1},{1,2},{2,3},{3,4},{4,5},{5,6},{6,7},{7,8},{8,9},{9,10},{10,1... | collective-permute-start | bytes 786440 | tf_op jit(solution)/shard_map/while/body/eval_jaxpr/ppermute | solution.py:24
  394.3 11.1 %collective-permute-start.1 = (f32[4,64,256]{1,0,2:T(4,128)S(1)}, f32[4,64,256]{1,0,2:T(4,128)S(1)}, u32[]{:S(2)}, u32[]{:S(2)}) collective-permute-start(f32[4,64,256]{1,0,2:T(4,128)S(1)} %get-tuple-element.312), channel_id=1, source_target_pairs={{1,0},{2,1},{3,2},{4,3},{5,4},{6,5},{7,6},{8,7},{9,8},{10,9},{11,1... | collective-permute-start | bytes 786440 | tf_op jit(solution)/shard_map/while/body/eval_jaxpr/ppermute | solution.py:25
  395.6 12.0 %collective-permute-start = (f32[4,64,256]{1,0,2:T(4,128)S(1)}, f32[4,64,256]{1,0,2:T(4,128)}, u32[]{:S(2)}, u32[]{:S(2)}) collective-permute-start(f32[4,64,256]{1,0,2:T(4,128)S(1)} %get-tuple-element.311), channel_id=1, source_target_pairs={{0,1},{1,2},{2,3},{3,4},{4,5},{5,6},{6,7},{7,8},{8,9},{9,10},{10,1... | collective-permute-start | bytes 786440 | tf_op jit(solution)/shard_map/while/body/eval_jaxpr/ppermute | solution.py:24
  426.6 12.3 %collective-permute-start.1 = (f32[4,64,256]{1,0,2:T(4,128)S(1)}, f32[4,64,256]{1,0,2:T(4,128)S(1)}, u32[]{:S(2)}, u32[]{:S(2)}) collective-permute-start(f32[4,64,256]{1,0,2:T(4,128)S(1)} %get-tuple-element.312), channel_id=1, source_target_pairs={{1,0},{2,1},{3,2},{4,3},{5,4},{6,5},{7,6},{8,7},{9,8},{10,9},{11,1... | collective-permute-start | bytes 786440 | tf_op jit(solution)/shard_map/while/body/eval_jaxpr/ppermute | solution.py:25
  427.9 13.2 %collective-permute-start = (f32[4,64,256]{1,0,2:T(4,128)S(1)}, f32[4,64,256]{1,0,2:T(4,128)}, u32[]{:S(2)}, u32[]{:S(2)}) collective-permute-start(f32[4,64,256]{1,0,2:T(4,128)S(1)} %get-tuple-element.311), channel_id=1, source_target_pairs={{0,1},{1,2},{2,3},{3,4},{4,5},{5,6},{6,7},{7,8},{8,9},{9,10},{10,1... | collective-permute-start | bytes 786440 | tf_op jit(solution)/shard_map/while/body/eval_jaxpr/ppermute | solution.py:24
  460.1 13.4 %collective-permute-start.1 = (f32[4,64,256]{1,0,2:T(4,128)S(1)}, f32[4,64,256]{1,0,2:T(4,128)S(1)}, u32[]{:S(2)}, u32[]{:S(2)}) collective-permute-start(f32[4,64,256]{1,0,2:T(4,128)S(1)} %get-tuple-element.312), channel_id=1, source_target_pairs={{1,0},{2,1},{3,2},{4,3},{5,4},{6,5},{7,6},{8,7},{9,8},{10,9},{11,1... | collective-permute-start | bytes 786440 | tf_op jit(solution)/shard_map/while/body/eval_jaxpr/ppermute | solution.py:25
  461.4 14.2 %collective-permute-start = (f32[4,64,256]{1,0,2:T(4,128)S(1)}, f32[4,64,256]{1,0,2:T(4,128)}, u32[]{:S(2)}, u32[]{:S(2)}) collective-permute-start(f32[4,64,256]{1,0,2:T(4,128)S(1)} %get-tuple-element.311), channel_id=1, source_target_pairs={{0,1},{1,2},{2,3},{3,4},{4,5},{5,6},{6,7},{7,8},{8,9},{9,10},{10,1... | collective-permute-start | bytes 786440 | tf_op jit(solution)/shard_map/while/body/eval_jaxpr/ppermute | solution.py:24
  494.7 14.4 %collective-permute-start.1 = (f32[4,64,256]{1,0,2:T(4,128)S(1)}, f32[4,64,256]{1,0,2:T(4,128)S(1)}, u32[]{:S(2)}, u32[]{:S(2)}) collective-permute-start(f32[4,64,256]{1,0,2:T(4,128)S(1)} %get-tuple-element.312), channel_id=1, source_target_pairs={{1,0},{2,1},{3,2},{4,3},{5,4},{6,5},{7,6},{8,7},{9,8},{10,9},{11,1... | collective-permute-start | bytes 786440 | tf_op jit(solution)/shard_map/while/body/eval_jaxpr/ppermute | solution.py:25
  496.0 15.2 %collective-permute-start = (f32[4,64,256]{1,0,2:T(4,128)S(1)}, f32[4,64,256]{1,0,2:T(4,128)}, u32[]{:S(2)}, u32[]{:S(2)}) collective-permute-start(f32[4,64,256]{1,0,2:T(4,128)S(1)} %get-tuple-element.311), channel_id=1, source_target_pairs={{0,1},{1,2},{2,3},{3,4},{4,5},{5,6},{6,7},{7,8},{8,9},{9,10},{10,1... | collective-permute-start | bytes 786440 | tf_op jit(solution)/shard_map/while/body/eval_jaxpr/ppermute | solution.py:24
  530.2 15.4 %collective-permute-start.1 = (f32[4,64,256]{1,0,2:T(4,128)S(1)}, f32[4,64,256]{1,0,2:T(4,128)S(1)}, u32[]{:S(2)}, u32[]{:S(2)}) collective-permute-start(f32[4,64,256]{1,0,2:T(4,128)S(1)} %get-tuple-element.312), channel_id=1, source_target_pairs={{1,0},{2,1},{3,2},{4,3},{5,4},{6,5},{7,6},{8,7},{9,8},{10,9},{11,1... | collective-permute-start | bytes 786440 | tf_op jit(solution)/shard_map/while/body/eval_jaxpr/ppermute | solution.py:25
  531.5 16.3 %collective-permute-start = (f32[4,64,256]{1,0,2:T(4,128)S(1)}, f32[4,64,256]{1,0,2:T(4,128)}, u32[]{:S(2)}, u32[]{:S(2)}) collective-permute-start(f32[4,64,256]{1,0,2:T(4,128)S(1)} %get-tuple-element.311), channel_id=1, source_target_pairs={{0,1},{1,2},{2,3},{3,4},{4,5},{5,6},{6,7},{7,8},{8,9},{9,10},{10,1... | collective-permute-start | bytes 786440 | tf_op jit(solution)/shard_map/while/body/eval_jaxpr/ppermute | solution.py:24
  566.8 17.9 %collective-permute-start.1 = (f32[4,64,256]{1,0,2:T(4,128)S(1)}, f32[4,64,256]{1,0,2:T(4,128)S(1)}, u32[]{:S(2)}, u32[]{:S(2)}) collective-permute-start(f32[4,64,256]{1,0,2:T(4,128)S(1)} %get-tuple-element.312), channel_id=1, source_target_pairs={{1,0},{2,1},{3,2},{4,3},{5,4},{6,5},{7,6},{8,7},{9,8},{10,9},{11,1... | collective-permute-start | bytes 786440 | tf_op jit(solution)/shard_map/while/body/eval_jaxpr/ppermute | solution.py:25
  568.1 18.7 %collective-permute-start = (f32[4,64,256]{1,0,2:T(4,128)S(1)}, f32[4,64,256]{1,0,2:T(4,128)}, u32[]{:S(2)}, u32[]{:S(2)}) collective-permute-start(f32[4,64,256]{1,0,2:T(4,128)S(1)} %get-tuple-element.311), channel_id=1, source_target_pairs={{0,1},{1,2},{2,3},{3,4},{4,5},{5,6},{6,7},{7,8},{8,9},{9,10},{10,1... | collective-permute-start | bytes 786440 | tf_op jit(solution)/shard_map/while/body/eval_jaxpr/ppermute | solution.py:24
  605.8 17.3 %collective-permute-start.1 = (f32[4,64,256]{1,0,2:T(4,128)S(1)}, f32[4,64,256]{1,0,2:T(4,128)S(1)}, u32[]{:S(2)}, u32[]{:S(2)}) collective-permute-start(f32[4,64,256]{1,0,2:T(4,128)S(1)} %get-tuple-element.312), channel_id=1, source_target_pairs={{1,0},{2,1},{3,2},{4,3},{5,4},{6,5},{7,6},{8,7},{9,8},{10,9},{11,1... | collective-permute-start | bytes 786440 | tf_op jit(solution)/shard_map/while/body/eval_jaxpr/ppermute | solution.py:25
  607.1 18.1 %collective-permute-start = (f32[4,64,256]{1,0,2:T(4,128)S(1)}, f32[4,64,256]{1,0,2:T(4,128)}, u32[]{:S(2)}, u32[]{:S(2)}) collective-permute-start(f32[4,64,256]{1,0,2:T(4,128)S(1)} %get-tuple-element.311), channel_id=1, source_target_pairs={{0,1},{1,2},{2,3},{3,4},{4,5},{5,6},{6,7},{7,8},{8,9},{9,10},{10,1... | collective-permute-start | bytes 786440 | tf_op jit(solution)/shard_map/while/body/eval_jaxpr/ppermute | solution.py:24
  644.3 15.6 %collective-permute-start.1 = (f32[4,64,256]{1,0,2:T(4,128)S(1)}, f32[4,64,256]{1,0,2:T(4,128)S(1)}, u32[]{:S(2)}, u32[]{:S(2)}) collective-permute-start(f32[4,64,256]{1,0,2:T(4,128)S(1)} %get-tuple-element.312), channel_id=1, source_target_pairs={{1,0},{2,1},{3,2},{4,3},{5,4},{6,5},{7,6},{8,7},{9,8},{10,9},{11,1... | collective-permute-start | bytes 786440 | tf_op jit(solution)/shard_map/while/body/eval_jaxpr/ppermute | solution.py:25
  645.6 16.5 %collective-permute-start = (f32[4,64,256]{1,0,2:T(4,128)S(1)}, f32[4,64,256]{1,0,2:T(4,128)}, u32[]{:S(2)}, u32[]{:S(2)}) collective-permute-start(f32[4,64,256]{1,0,2:T(4,128)S(1)} %get-tuple-element.311), channel_id=1, source_target_pairs={{0,1},{1,2},{2,3},{3,4},{4,5},{5,6},{6,7},{7,8},{8,9},{9,10},{10,1... | collective-permute-start | bytes 786440 | tf_op jit(solution)/shard_map/while/body/eval_jaxpr/ppermute | solution.py:24
  681.1 13.4 %collective-permute-start.1 = (f32[4,64,256]{1,0,2:T(4,128)S(1)}, f32[4,64,256]{1,0,2:T(4,128)S(1)}, u32[]{:S(2)}, u32[]{:S(2)}) collective-permute-start(f32[4,64,256]{1,0,2:T(4,128)S(1)} %get-tuple-element.312), channel_id=1, source_target_pairs={{1,0},{2,1},{3,2},{4,3},{5,4},{6,5},{7,6},{8,7},{9,8},{10,9},{11,1... | collective-permute-start | bytes 786440 | tf_op jit(solution)/shard_map/while/body/eval_jaxpr/ppermute | solution.py:25
  682.4 14.2 %collective-permute-start = (f32[4,64,256]{1,0,2:T(4,128)S(1)}, f32[4,64,256]{1,0,2:T(4,128)}, u32[]{:S(2)}, u32[]{:S(2)}) collective-permute-start(f32[4,64,256]{1,0,2:T(4,128)S(1)} %get-tuple-element.311), channel_id=1, source_target_pairs={{0,1},{1,2},{2,3},{3,4},{4,5},{5,6},{6,7},{7,8},{8,9},{9,10},{10,1... | collective-permute-start | bytes 786440 | tf_op jit(solution)/shard_map/while/body/eval_jaxpr/ppermute | solution.py:24
  (64 other events, 665.2 us)
Sparse Core Ops, SparseCore 0:
  717.9 109.4 reduce-scatter.1
